TPU v7x, 256 devices: a whole 4x4x8 slice. The times are simulated.
256 devices in a mesh: rep: 16 (over x, z_hi), tp: 16 (over z_lo, y, core).
Axes of the slice: x: 4, y: 4, z: 8 (z_hi: 4, z_lo: 2; z = z_hi * 2 + z_lo), core: 2. Of those that a mesh axis runs over, the one named last changes fastest.
Arguments:
- hidden: bfloat16 [32768, 8192], P('rep', 'tp'), may hold values from -0.0625 to 0.0625
- target: bfloat16 [32768, 1024], P('rep'), may hold values from -6 to 6
- inner_weight: bfloat16 [16, 8192, 1024], P('rep', 'tp'), as said below
- first_moment: float32 [16, 8192, 1024], P('rep', 'tp'), may hold values from -1.5 to 1.5
- second_moment: float32 [16, 8192, 1024], P('rep', 'tp'), may hold values from 0.001 to 0.01
- anchor: float32 [16, 512, 1024], P('tp', 'rep')
- outer_momentum: float32 [16, 512, 1024], P('tp', 'rep'), may hold values from -1.5 to 1.5
Outputs:
- fragment: bfloat16 [8192, 1024], P('tp')
- momentum_new: float32 [16, 512, 1024], P('tp', 'rep')
Inputs may be any that keep to these rules, and one draw needn't show every extreme that they name: `inner_weight`: each replica's inner weights are the anchor plus a drift of their own.
All inputs are finite; a program needn't handle non-finite values.
Results may differ from a plain program's by a relative error of at most 0.0017.
Values may be sent and summed in bfloat16 or wider, within the bound.
No kernel may reach another device: no remote copies, remote signals or barrier semaphores. Data moves between devices by JAX's collectives and lax.ppermute only.
A program may use at most 64 MiB of HBM per device.

v0:
```python
import jax
import jax.numpy as jnp
from jax import lax
from jax.sharding import PartitionSpec as P

beta_one = 0.9
beta_two = 0.999
inner_rate = 0.2
decay_rate = 0.1
outer_rate = 0.7
outer_mu = 0.9
adam_eps = 1e-08


def local(hidden, target, inner_weight, first_moment, second_moment, anchor, outer_momentum):
    weight = inner_weight[0]
    partial_value = jnp.dot(hidden, weight, preferred_element_type=jnp.float32)
    summed = lax.psum_scatter(
        partial_value.astype(jnp.bfloat16), "tp", scatter_dimension=0, tiled=True
    ).astype(jnp.float32)
    count = summed.shape[0]
    goal = lax.dynamic_slice_in_dim(target, lax.axis_index("tp") * count, count, 0)
    residual = (summed - goal.astype(jnp.float32)).astype(jnp.bfloat16)
    grad = lax.dot_general(
        hidden,
        lax.all_gather(residual, "tp", axis=0, tiled=True),
        (((0,), (0,)), ((), ())),
        preferred_element_type=jnp.float32,
    )
    moment_one = beta_one * first_moment[0] + (1.0 - beta_one) * grad
    moment_two = beta_two * second_moment[0] + (1.0 - beta_two) * grad * grad
    corr_one = 1.0 - beta_one**3
    corr_two = 1.0 - beta_two**3
    weight_f = weight.astype(jnp.float32)
    step_dir = moment_one / corr_one / (jnp.sqrt(moment_two / corr_two) + adam_eps)
    updated = weight_f - inner_rate * (step_dir + decay_rate * weight_f)
    replicas = lax.axis_size("rep")
    replica_mean = lax.psum_scatter(updated, "rep", scatter_dimension=0, tiled=True) / replicas
    anchor_rows = anchor[0]
    delta = anchor_rows - replica_mean
    momentum_new = outer_mu * outer_momentum[0] + delta
    piece = (anchor_rows - outer_rate * (delta + outer_mu * momentum_new)).astype(jnp.bfloat16)
    fragment = lax.all_gather(piece, "rep", axis=0, tiled=True)
    return (fragment, momentum_new[None])


def solution(mesh):
    placed = (
        P("rep", "tp"),
        P("rep", None),
        P("rep", "tp", None),
        P("rep", "tp", None),
        P("rep", "tp", None),
        P("tp", "rep", None),
        P("tp", "rep", None),
    )
    return jax.shard_map(
        local,
        mesh=mesh,
        in_specs=placed,
        out_specs=(P("tp", None), P("tp", "rep", None)),
        check_vma=False,
    )
```

profile of v0, /device:TPU:8, one launch (start us, length us, event | category | flops | bytes accessed | tf_op | source)
XLA Modules:
  0.0 292.7 jit_solution(12165705362500873506)
XLA Ops:
  7.2 0.0 copy-start
  7.2 0.0 reduce-scatter.5.cloned.1.call-start
  7.2 1.5 copy-done
  8.8 5.5 %convolution_convert_fusion = bf16[2048,1024]{1,0:T(8,128)(2,1)} fusion(bf16[2048,512]{1,0:T(8,128)(2,1)S(1)} %copy-done, bf16[1,512,1024]{2,1,0:T(8,128)(2,1)} %param.9), kind=kOutput, calls=%fused_computation | convolution fusion | flops 2149580800 | bytes 7340032 | tf_op jit(solution)/shard_map/dot_general | solution.py:17
  14.3 0.0 reduce-scatter.5.cloned.1.call-update
  14.3 0.0 all-gather.3.cloned.1.call-start
  14.4 68.8 %reduce-scatter.5.cloned.1.call-done = bf16[128,1024]{1,0:T(8,128)(2,1)} async-done(((bf16[2048,1024]{1,0:T(8,128)(2,1)}), bf16[128,1024]{1,0:T(8,128)(2,1)}) %reduce-scatter.5.cloned.1.call-update) | async-done | bytes 262160 | tf_op jit(solution)/shard_map/reduce_scatter | solution.py:18
  83.2 1.8 subtract_convert_fusion
  85.0 0.0 all-gather.3.cloned.1.call-update
  85.1 0.0 reduce-scatter.7.cloned.1.call-start
  85.1 0.0 copy-done.1
  85.1 1.3 copy.17
  86.4 2.9 copy.18
  89.3 3.0 %copy.19 = f32[1,512,1024]{1,2,0:T(8,128)} copy(f32[1,512,1024]{2,1,0:T(8,128)} %param.11) | data formatting | bytes 4194304 | tf_op args[4]
  92.4 34.4 %all-gather.3.cloned.1.call-done = bf16[2048,1024]{1,0:T(8,128)(2,1)} async-done(((bf16[128,1024]{1,0:T(8,128)(2,1)}), bf16[2048,1024]{1,0:T(8,128)(2,1)}) %all-gather.3.cloned.1.call-update) | async-done | bytes 4194320 | tf_op jit(solution)/shard_map/all_gather | solution.py:26
  126.8 0.0 copy-done.2
  126.8 8.6 %convert_subtract_fusion = f32[512,1024]{0,1:T(8,128)} fusion(f32[1,512,1024]{1,2,0:T(8,128)} %copy.19, f32[1,512,1024]{1,2,0:T(8,128)} %copy.18, bf16[2048,1024]{1,0:T(8,128)(2,1)} %all-gather.3.cloned.1.call-done, bf16[2048,512]{1,0:T(8,128)(2,1)S(1)} %copy-done, bf16[1,512,1024]{1,2,0:T(8,128)(2,1)S(1)} %copy-done.2), kind=kOutput, calls=%fused_computation.2 | convolution fusion | flops 2155872256 | bytes 13631488 | tf_op jit(solution)/shard_map/dot_general | solution.py:24
  135.3 2.9 copy.23
  138.3 0.0 reduce-scatter.7.cloned.1.call-update
  138.3 0.0 all-gather.5.cloned.1.call-start
  138.3 0.8 copy-done.3
  139.2 0.2 copy.16
  139.4 0.0 copy-done.4
  139.4 1.0 copy.20
  140.4 88.4 %reduce-scatter.7.cloned.1.call-done = f32[32,1024]{1,0:T(8,128)} async-done(((f32[512,1024]{1,0:T(8,128)}), f32[32,1024]{1,0:T(8,128)}) %reduce-scatter.7.cloned.1.call-update) | async-done | bytes 131088
  228.8 1.9 copy.24
  230.7 1.4 fusion.11
  232.1 0.8 copy.21
  232.8 0.0 all-gather.5.cloned.1.call-update
  232.9 0.8 copy.22
  233.7 50.2 %all-gather.5.cloned.1.call-done = bf16[512,1024]{1,0:T(8,128)(2,1)} async-done(((bf16[32,1024]{1,0:T(8,128)(2,1)}), bf16[512,1024]{1,0:T(8,128)(2,1)}) %all-gather.5.cloned.1.call-update) | async-done | bytes 1048592 | tf_op jit(solution)/shard_map/all_gather | solution.py:43
  283.9 2.3 copy.26
  (4 shorter events, 0.0 us)
Async XLA Ops:
  7.2 1.6 copy-start
  7.2 76.0 %reduce-scatter.5.cloned.1.call-start = ((), (), s32[]{:S(2)}) async-start(), calls=%async_computation.2 | async-start | bytes 4456448 | tf_op jit(solution)/shard_map/reduce_scatter | solution.py:18
  14.3 70.8 %copy-start.1 = (bf16[1,512,1024]{2,1,0:T(8,128)(2,1)S(1)}, bf16[1,512,1024]{2,1,0:T(8,128)(2,1)}, u32[]{:S(2)}) copy-start(bf16[1,512,1024]{2,1,0:T(8,128)(2,1)} %param.9) | copy-start | bytes 3145732
  14.3 112.5 %all-gather.3.cloned.1.call-start = ((), (), s32[]{:S(2)}) async-start(), calls=%async_computation.3 | async-start | bytes 4456448 | tf_op jit(solution)/shard_map/all_gather | solution.py:26
  85.1 143.8 %reduce-scatter.7.cloned.1.call-start = ((), (), s32[]{:S(2)}) async-start(), calls=%async_computation.5 | async-start | bytes 2228224
  89.3 37.4 %copy-start.2 = (bf16[1,512,1024]{1,2,0:T(8,128)(2,1)S(1)}, bf16[1,512,1024]{1,2,0:T(8,128)(2,1)}, u32[]{:S(2)}) copy-start(bf16[1,512,1024]{1,2,0:T(8,128)(2,1)} %copy.17) | copy-start | bytes 3145732
  138.3 0.9 copy-start.3
  138.3 1.1 copy-start.4
  138.3 145.6 %all-gather.5.cloned.1.call-start = ((), (), s32[]{:S(2)}) async-start(), calls=%async_computation.4 | async-start | bytes 1114112 | tf_op jit(solution)/shard_map/all_gather | solution.py:43
Sparse Core Ops, SparseCore 0:
  14.4 68.7 reduce-scatter.4
  85.2 41.5 all-gather.2
  138.4 90.3 reduce-scatter.6
  233.0 50.9 all-gather.4
where the time goes:
time: 293 us
  waiting for transfers between devices  242 us (83%)
  local copies, waits for them, and re-layouts  19.5 us (7%)
  matrix products  14.1 us (5%)
  between operations  13.8 us (5%)
  other arithmetic  3.19 us (1%)
    unnamed x5, waiting for transfers between devices  88.5 us
    reduce_scatter x1, waiting for transfers between devices, local(): lax.psum_scatter(partial_value.astype(jnp.bfloat16), 'tp', scatter_dimens...  68.8 us
    all_gather x1, waiting for transfers between devices, local(): fragment = lax.all_gather(piece, 'rep', axis=0, tiled=True)  50.2 us
    all_gather x1, waiting for transfers between devices, local(): lax.all_gather(residual, 'tp', axis=0, tiled=True)  34.4 us
    unnamed x19, local copies, waits for them, and re-layouts  18.7 us
    dot_general x1, matrix products, local(): lax.dot_general(hidden, lax.all_gather(residual, 'tp', axis=0, tiled=True...  8.58 us
  transfers between devices with their start and end apart: 4, of which 4 were waited for; matrix products, arithmetic and copies ran while one was open for 3% of the time, Pallas kernels for 0%

commit v1 on v0

--- a/solution.py
+++ b/solution.py
@@ -12,6 +12,11 @@
 adam_eps = 1e-08
 
 
+def gather_over(x, axis, dim):
+    repeated = jnp.stack([x] * lax.axis_size(axis))
+    return jnp.concatenate(lax.all_to_all(repeated, axis, 0, 0), axis=dim)
+
+
 def local(hidden, target, inner_weight, first_moment, second_moment, anchor, outer_momentum):
     weight = inner_weight[0]
     partial_value = jnp.dot(hidden, weight, preferred_element_type=jnp.float32)
@@ -23,7 +28,7 @@
     residual = (summed - goal.astype(jnp.float32)).astype(jnp.bfloat16)
     grad = lax.dot_general(
         hidden,
-        lax.all_gather(residual, "tp", axis=0, tiled=True),
+        gather_over(residual, "tp", 0),
         (((0,), (0,)), ((), ())),
         preferred_element_type=jnp.float32,
     )

time: 293 us -> 323 us (1.10)
  waiting for transfers between devices: 242 us -> 261 us
  starting transfers between devices: 0.16 us -> 9.15 us
    all_to_all x0 -> x1, waiting for transfers between devices: none -> 52.5 us  [gather_over(): return jnp.concatenate(lax.all_to_all(repeated, axis, 0, 0), axis=dim)]
    all_gather x1 -> x0, waiting for transfers between devices: 34.4 us -> none  [local(): lax.all_gather(residual, 'tp', axis=0, tiled=True)]
    all_to_all x0 -> x1, starting transfers between devices: none -> 9.03 us  [gather_over(): return jnp.concatenate(lax.all_to_all(repeated, axis, 0, 0), axis=dim)]
    unnamed x5 -> x4, waiting for transfers between devices: 88.5 us -> 89.6 us
where the time goes in v1:
time: 323 us
  waiting for transfers between devices  261 us (81%)
  local copies, waits for them, and re-layouts  22 us (7%)
  matrix products  14.1 us (4%)
  between operations  13.8 us (4%)
  starting transfers between devices  9.15 us (3%)
    unnamed x4, waiting for transfers between devices  89.6 us
    reduce_scatter x1, waiting for transfers between devices, local(): lax.psum_scatter(partial_value.astype(jnp.bfloat16), 'tp', scatter_dimens...  68.9 us
    all_to_all x1, waiting for transfers between devices, gather_over(): return jnp.concatenate(lax.all_to_all(repeated, axis, 0, 0), axis=dim)  52.5 us
    all_gather x1, waiting for transfers between devices, local(): fragment = lax.all_gather(piece, 'rep', axis=0, tiled=True)  50.3 us
    unnamed x19, local copies, waits for them, and re-layouts  18.7 us
    all_to_all x1, starting transfers between devices, gather_over(): return jnp.concatenate(lax.all_to_all(repeated, axis, 0, 0), axis=dim)  9.03 us
    dot_general x1, matrix products, local(): lax.dot_general(hidden, gather_over(residual, 'tp', 0), (((0,), (0,)), ((...  8.57 us
  transfers between devices with their start and end apart: 4, of which 4 were waited for; matrix products, arithmetic and copies ran while one was open for 3% of the time, Pallas kernels for 0%

profile of v1, /device:TPU:8, one launch (start us, length us, event | category | flops | bytes accessed | tf_op | source)
XLA Modules:
  0.0 322.7 jit_solution(13245996481023785322)
XLA Ops:
  7.2 0.0 copy-start
  7.2 0.0 reduce-scatter.5.cloned.1.call-start
  7.2 1.5 copy-done
  8.8 5.5 %convolution_convert_fusion = bf16[2048,1024]{1,0:T(8,128)(2,1)} fusion(bf16[2048,512]{1,0:T(8,128)(2,1)S(1)} %copy-done, bf16[1,512,1024]{2,1,0:T(8,128)(2,1)} %param.9), kind=kOutput, calls=%fused_computation | convolution fusion | flops 2149580800 | bytes 7340032 | tf_op jit(solution)/shard_map/dot_general | solution.py:22
  14.3 0.0 reduce-scatter.5.cloned.1.call-update
  14.3 68.9 %reduce-scatter.5.cloned.1.call-done = bf16[128,1024]{1,0:T(8,128)(2,1)} async-done(((bf16[2048,1024]{1,0:T(8,128)(2,1)}), bf16[128,1024]{1,0:T(8,128)(2,1)}) %reduce-scatter.5.cloned.1.call-update) | async-done | bytes 262160 | tf_op jit(solution)/shard_map/reduce_scatter | solution.py:23
  83.2 1.1 subtract_convert_fusion
  84.3 2.5 stack.2
  86.8 9.0 %all-to-all-start = ((bf16[16,128,1024]{2,1,0:T(8,128)(2,1)}), bf16[16,128,1024]{2,1,0:T(8,128)(2,1)}, u32[]{:S(2)}, u32[]{:S(2)}) async-start(bf16[16,128,1024]{2,1,0:T(8,128)(2,1)} %stack.2), calls=%async_computation.1 | async-start | bytes 8388608 | tf_op jit(solution)/shard_map/all_to_all | solution.py:17
  95.8 0.0 reduce-scatter.7.cloned.1.call-start
  95.9 0.0 copy-done.1
  95.9 1.3 copy.17
  97.2 2.9 copy.18
  100.2 3.0 copy.19
  103.1 52.5 %all-to-all-done = bf16[16,128,1024]{2,1,0:T(8,128)(2,1)} async-done(((bf16[16,128,1024]{2,1,0:T(8,128)(2,1)}), bf16[16,128,1024]{2,1,0:T(8,128)(2,1)}, u32[]{:S(2)}, u32[]{:S(2)}) %all-to-all-start) | async-done | bytes 4194336 | tf_op jit(solution)/shard_map/all_to_all | solution.py:17
  155.6 0.0 copy-done.2
  155.6 8.6 %convert_subtract_fusion = f32[512,1024]{0,1:T(8,128)} fusion(f32[1,512,1024]{1,2,0:T(8,128)} %copy.19, f32[1,512,1024]{1,2,0:T(8,128)} %copy.18, bf16[2048,1024]{1,0:T(8,128)(2,1)} %bitcast.3, bf16[2048,512]{1,0:T(8,128)(2,1)S(1)} %copy-done, bf16[1,512,1024]{1,2,0:T(8,128)(2,1)S(1)} %copy-done.2), kind=kOutput, calls=%fused_computation.2 | convolution fusion | flops 2155872256 | bytes 13631488 | tf_op jit(solution)/shard_map/dot_general | solution.py:29
  164.2 2.9 copy.23
  167.1 0.0 reduce-scatter.7.cloned.1.call-update
  167.1 0.0 all-gather.2.cloned.1.call-start
  167.2 0.8 copy-done.3
  168.0 0.2 copy.16
  168.2 0.0 copy-done.4
  168.2 1.0 copy.20
  169.2 89.5 %reduce-scatter.7.cloned.1.call-done = f32[32,1024]{1,0:T(8,128)} async-done(((f32[512,1024]{1,0:T(8,128)}), f32[32,1024]{1,0:T(8,128)}) %reduce-scatter.7.cloned.1.call-update) | async-done | bytes 131088
  258.7 1.9 copy.24
  260.6 1.4 fusion.11
  262.0 0.8 copy.21
  262.8 0.0 all-gather.2.cloned.1.call-update
  262.8 0.8 copy.22
  263.6 50.3 %all-gather.2.cloned.1.call-done = bf16[512,1024]{1,0:T(8,128)(2,1)} async-done(((bf16[32,1024]{1,0:T(8,128)(2,1)}), bf16[512,1024]{1,0:T(8,128)(2,1)}) %all-gather.2.cloned.1.call-update) | async-done | bytes 1048592 | tf_op jit(solution)/shard_map/all_gather | solution.py:48
  313.9 2.3 copy.26
  (4 shorter events, 0.0 us)
Async XLA Ops:
  7.2 1.6 copy-start
  7.2 76.0 %reduce-scatter.5.cloned.1.call-start = ((), (), s32[]{:S(2)}) async-start(), calls=%async_computation.3 | async-start | bytes 4456448 | tf_op jit(solution)/shard_map/reduce_scatter | solution.py:23
  86.8 9.1 %copy-start.1 = (bf16[1,512,1024]{2,1,0:T(8,128)(2,1)S(1)}, bf16[1,512,1024]{2,1,0:T(8,128)(2,1)}, u32[]{:S(2)}) copy-start(bf16[1,512,1024]{2,1,0:T(8,128)(2,1)} %param.9) | copy-start | bytes 3145732
  86.8 68.8 %all-to-all-start = ((bf16[16,128,1024]{2,1,0:T(8,128)(2,1)}), bf16[16,128,1024]{2,1,0:T(8,128)(2,1)}, u32[]{:S(2)}, u32[]{:S(2)}) async-start(bf16[16,128,1024]{2,1,0:T(8,128)(2,1)} %stack.2), calls=%async_computation.1 | async-start | bytes 8388608 | tf_op jit(solution)/shard_map/all_to_all | solution.py:17
  95.8 162.9 %reduce-scatter.7.cloned.1.call-start = ((), (), s32[]{:S(2)}) async-start(), calls=%async_computation.5 | async-start | bytes 2228224
  100.2 55.5 %copy-start.2 = (bf16[1,512,1024]{1,2,0:T(8,128)(2,1)S(1)}, bf16[1,512,1024]{1,2,0:T(8,128)(2,1)}, u32[]{:S(2)}) copy-start(bf16[1,512,1024]{1,2,0:T(8,128)(2,1)} %copy.17) | copy-start | bytes 3145732
  167.1 0.9 copy-start.3
  167.1 1.1 copy-start.4
  167.1 146.8 %all-gather.2.cloned.1.call-start = ((), (), s32[]{:S(2)}) async-start(), calls=%async_computation.4 | async-start | bytes 1114112 | tf_op jit(solution)/shard_map/all_gather | solution.py:48
Sparse Core Ops, SparseCore 0:
  14.4 68.7 reduce-scatter.4
  167.2 91.4 reduce-scatter.6
  262.9 50.9 all-gather.1
